TPU v7x, 512 devices: a whole 4x4x16 slice. The times are simulated.
512 devices in a mesh: kv: 8 (over x, core), pool: 64 (over y, z).
Axes of the slice: x: 4, y: 4, z: 16, core: 2. Of those that a mesh axis runs over, the one named last changes fastest.
Arguments:
- hidden: bfloat16 [64, 2048], P('pool'), may hold values from -6 to 6
- norm_attn: bfloat16 [2048], replicated, may hold values from 0.099609375 to 1.8984375
- wq: bfloat16 [2048, 2048], P(None, 'kv'), may hold values from -0.125 to 0.125
- wkv: bfloat16 [2, 2048, 1024], P(None, None, 'kv'), may hold values from -0.125 to 0.125
- wo: bfloat16 [2048, 2048], P('kv'), may hold values from -0.125 to 0.125
- cache: bfloat16 [2, 1024, 128, 1024], P(None, 'pool', None, 'kv'), may hold values from -70 to 70, as said below
- slot_entry: int32 [1024], P('pool'), may hold values from -1 to 4095, as said below
- lengths: int32 [64], replicated, may hold values from 1 to 8192, as said below
- norm_mlp: bfloat16 [2048], replicated, may hold values from 0.099609375 to 1.8984375
- w_gate: bfloat16 [2048, 8192], P('pool', 'kv'), may hold values from -0.125 to 0.125
- w_up: bfloat16 [2048, 8192], P('pool', 'kv'), may hold values from -0.125 to 0.125
- w_down: bfloat16 [8192, 2048], P('kv', 'pool'), may hold values from -0.0625 to 0.0625
Outputs:
- output: bfloat16 [64, 2048], P('pool')
Inputs may be any that keep to these rules, and one draw needn't show every extreme that they name: slot_entry[s] is -1 for a free slot, else r * 64 + b: the slot holds block b of request r, that is its cached positions b * 128 to b * 128 + 127 that lie below lengths[r]. Every block of every request below ceil(lengths[r] / 128) sits in exactly one slot, anywhere in the pool; a holder's slots are its 16 entries. Its new token stands at position lengths[r]. `cache`: keys and values of the cached tokens, already rotated.
All inputs are finite; a program needn't handle non-finite values.
Results may differ from a plain program's by a relative error of at most 0.012.
The roundings to bfloat16 on the way count: a program that leaves them out, or rounds other values in their place, can miss the bound.
Values may be sent and summed in bfloat16 or wider, within the bound.
A program may use at most 64 MiB of HBM per device.

v0:
```python
import math
import jax
import jax.numpy as jnp
from jax import lax
from jax.sharding import PartitionSpec as P

QUERY_HEAD_COUNT = 16
KEY_VALUE_HEADS = 8
HEAD_SIZE = 128
NEGATIVE = -1e30
EPSILON = 1e-05
ROPE_BASE = 1000000.0


def narrow_rows(tensor):
    return lax.optimization_barrier(tensor.astype(jnp.bfloat16))


def rms_scale(inputs, gain_vec):
    widened = inputs.astype(jnp.float32)
    mean_square = jnp.mean(widened * widened, axis=-1, keepdims=True)
    return narrow_rows(widened * lax.rsqrt(mean_square + EPSILON) * gain_vec.astype(jnp.float32))


def rotate(vectors, positions):
    head_width = vectors.shape[-1]
    halfway = head_width // 2
    frequency = jnp.exp(
        jnp.arange(halfway, dtype=jnp.float32) * (-2.0 * math.log(ROPE_BASE) / head_width)
    )
    angles = positions.astype(jnp.float32)[:, None] * frequency[None, :]
    cosine = jnp.cos(angles)[:, None, :]
    sine_of = jnp.sin(angles)[:, None, :]
    leading = vectors[..., :halfway]
    trailing = vectors[..., halfway:]
    return jnp.concatenate(
        [leading * cosine - trailing * sine_of, trailing * cosine + leading * sine_of], axis=-1
    )


def per_device(
    hidden, norm_attn, wq, wkv, wo, cache, slot_entry, lengths, norm_mlp, w_gate, w_up, w_down
):
    home_rows = hidden.shape[0]
    shared_heads = wkv.shape[2] // HEAD_SIZE
    queries_per_shared = QUERY_HEAD_COUNT // KEY_VALUE_HEADS
    query_heads = shared_heads * queries_per_shared
    home_index = lax.axis_index("pool")
    max_blocks = slot_entry.shape[0] * lax.axis_size("pool") // 16
    positions = lax.dynamic_slice_in_dim(lengths, home_index * home_rows, home_rows)
    normed_input = rms_scale(hidden, norm_attn)
    query_rows = jnp.dot(normed_input, wq, preferred_element_type=jnp.float32).reshape(
        home_rows, query_heads, HEAD_SIZE
    )
    query_rows = narrow_rows(rotate(query_rows, positions) * HEAD_SIZE ** (-0.5))
    fresh_keys = jnp.dot(normed_input, wkv[0], preferred_element_type=jnp.float32).reshape(
        home_rows, shared_heads, HEAD_SIZE
    )
    fresh_keys = narrow_rows(rotate(fresh_keys, positions))
    fresh_values = narrow_rows(
        jnp.dot(normed_input, wkv[1], preferred_element_type=jnp.float32)
    ).reshape(home_rows, shared_heads, HEAD_SIZE)
    every_query = lax.all_gather(
        query_rows.reshape(home_rows, query_heads * HEAD_SIZE), "pool", axis=0, tiled=True
    )
    request_list = every_query.shape[0]
    every_query = every_query.reshape(request_list, shared_heads, queries_per_shared, HEAD_SIZE)
    slot_count = slot_entry.shape[0]
    block_len = cache.shape[2]
    live_slot = slot_entry >= 0
    owners = jnp.where(live_slot, slot_entry // max_blocks, 0)
    block_index = jnp.where(live_slot, slot_entry % max_blocks, 0)
    position = block_index[:, None] * block_len + jnp.arange(block_len, dtype=jnp.int32)[None, :]
    in_range = live_slot[:, None] & (position < lengths[owners][:, None])
    token_owner = jnp.where(in_range, owners[:, None], -1).reshape(1, slot_count * block_len)
    keys = cache[0].reshape(slot_count * block_len, HEAD_SIZE)
    values = cache[1].reshape(slot_count * block_len, HEAD_SIZE)
    stacked = every_query.reshape(request_list, query_heads, HEAD_SIZE).transpose(1, 0, 2)
    stacked = stacked.reshape(query_heads * request_list, HEAD_SIZE)
    scores = lax.dot_general(
        stacked, keys, (((1,), (1,)), ((), ())), preferred_element_type=jnp.float32
    )
    row_owner = jnp.tile(jnp.arange(request_list, dtype=jnp.int32), query_heads)[:, None]
    taken = row_owner == token_owner
    scores = jnp.where(taken, scores, NEGATIVE)
    row_max = jnp.max(scores, axis=-1, keepdims=True)
    raised = jnp.where(taken, jnp.exp(scores - row_max), 0.0)
    row_total = jnp.sum(raised, axis=-1, keepdims=True)
    row_out = jnp.dot(raised.astype(jnp.bfloat16), values, preferred_element_type=jnp.float32)
    packed = (
        jnp.concatenate(
            [
                row_out,
                jnp.broadcast_to(row_max, (row_max.shape[0], 64)),
                jnp.broadcast_to(row_total, (row_max.shape[0], 64)),
            ],
            axis=1,
        )
        .reshape(query_heads, request_list, 256)
        .transpose(1, 0, 2)
        .reshape(request_list, query_heads * 256)
    )
    arrived = lax.all_to_all(packed, "pool", split_axis=0, concat_axis=0, tiled=True)
    arrived = arrived.reshape(request_list, query_heads, 256)
    every_max = arrived[:, :, 128]
    part_max = jnp.max(every_max, axis=0, keepdims=True)
    factor = jnp.exp(every_max - part_max)
    part_total = jnp.sum(factor * arrived[:, :, 192], axis=0, keepdims=True)
    part_out = jnp.sum(factor[:, :, None] * arrived[:, :, :128], axis=0).reshape(
        1, query_heads * HEAD_SIZE
    )
    own_query = query_rows.reshape(home_rows, shared_heads, queries_per_shared, HEAD_SIZE).astype(
        jnp.float32
    )
    new_score = jnp.sum(own_query * fresh_keys.astype(jnp.float32)[:, :, None, :], axis=-1).reshape(
        home_rows, query_heads
    )
    highest = jnp.maximum(part_max, new_score)
    old_scale = jnp.exp(part_max - highest)
    new_scale = jnp.exp(new_score - highest)
    weight_sum = part_total * old_scale + new_scale
    new_term = (
        new_scale.reshape(home_rows, shared_heads, queries_per_shared)[..., None]
        * fresh_values.astype(jnp.float32)[:, :, None, :]
    )
    combined = part_out.reshape(home_rows, query_heads, HEAD_SIZE) * old_scale[
        ..., None
    ] + new_term.reshape(home_rows, query_heads, HEAD_SIZE)
    attended = narrow_rows(combined / weight_sum[..., None]).reshape(
        home_rows, query_heads * HEAD_SIZE
    )
    projected = lax.psum(jnp.dot(attended, wo, preferred_element_type=jnp.float32), "kv")
    residual = narrow_rows(hidden.astype(jnp.float32) + projected)
    mlp_in = rms_scale(residual, norm_mlp)
    columns = lax.all_to_all(mlp_in, "pool", split_axis=1, concat_axis=0, tiled=True)
    hidden_width = w_gate.shape[1]
    gate_term = jnp.dot(columns, w_gate, preferred_element_type=jnp.float32)
    up_term = jnp.dot(columns, w_up, preferred_element_type=jnp.float32)
    sent = jnp.concatenate([gate_term, up_term], axis=1).astype(jnp.bfloat16)
    summed = jnp.sum(
        lax.all_to_all(sent, "pool", split_axis=0, concat_axis=0, tiled=True).astype(jnp.float32),
        axis=0,
        keepdims=True,
    )
    activation = narrow_rows(jax.nn.silu(summed[:, :hidden_width]) * summed[:, hidden_width:])
    projected_down = jnp.dot(
        lax.all_gather(activation, "pool", axis=0, tiled=True),
        w_down,
        preferred_element_type=jnp.float32,
    )
    mlp_out = narrow_rows(lax.psum(projected_down, "kv"))
    returned = lax.all_to_all(mlp_out, "pool", split_axis=0, concat_axis=1, tiled=True)
    return (residual.astype(jnp.float32) + returned.astype(jnp.float32)).astype(jnp.bfloat16)


def solution(mesh):
    return jax.shard_map(
        per_device,
        mesh=mesh,
        in_specs=(
            P("pool", None),
            P(),
            P(None, "kv"),
            P(None, None, "kv"),
            P("kv", None),
            P(None, "pool", None, "kv"),
            P("pool"),
            P(),
            P(),
            P("pool", "kv"),
            P("pool", "kv"),
            P("kv", "pool"),
        ),
        out_specs=P("pool", None),
        check_vma=False,
    )
```

profile of v0, /device:TPU:8, one launch (start us, length us, event | category | flops | bytes accessed | tf_op | source)
XLA Modules:
  0.0 311.4 jit_solution(4484563222303054181)
XLA Ops:
  0.0 0.7 copy-done.9
  0.8 0.6 copy-done.1
  1.5 0.6 dynamic_slice.3
  2.8 0.6 multiply_reduce_fusion.1
  4.1 1.5 fusion.4
  5.7 88.1 %all-gather = bf16[64,1,256]{2,1,0:T(2,128)(2,1)S(1)} all-gather(bf16[1,1,256]{2,1,0:T(2,128)(2,1)S(1)} %reshape.500), channel_id=1, replica_groups=mesh['kv'=8,'pool'=64] {'pool'}, dimensions={0}, use_global_device_ids=true | all-gather | bytes 33280 | tf_op jit(solution)/shard_map/all_gather | solution.py:63
  94.1 0.7 gather_fusion
  95.8 0.4 fusion.9
  96.5 0.8 all_to_all.40
  97.3 10.4 %all-to-all-start = ((f32[64,1,512]{2,1,0:T(1,128)}), f32[64,1,512]{2,1,0:T(1,128)S(1)}, u32[]{:S(2)}, u32[]{:S(2)}) async-start(f32[64,1,512]{2,1,0:T(1,128)} %all_to_all.40), calls=%async_computation | async-start | bytes 262144 | tf_op jit(solution)/shard_map/all_to_all | solution.py:103
  108.3 0.5 copy-done.8
  109.0 13.0 %all-to-all-done = f32[64,1,512]{2,1,0:T(1,128)S(1)} async-done(((f32[64,1,512]{2,1,0:T(1,128)}), f32[64,1,512]{2,1,0:T(1,128)S(1)}, u32[]{:S(2)}, u32[]{:S(2)}) %all-to-all-start) | async-done | bytes 131104 | tf_op jit(solution)/shard_map/all_to_all | solution.py:103
  123.6 12.6 %psum.14 = f32[1,2048]{1,0:T(1,128)S(1)} all-reduce(f32[1,2048]{1,0:T(1,128)S(1)} %fusion.53), channel_id=1, replica_groups=mesh['kv'=8,'pool'=64] {'kv'}, use_global_device_ids=true, to_apply=%region_7.8 | all-reduce | flops 2048 | bytes 16384 | tf_op jit(solution)/shard_map/psum | solution.py:132
  136.3 0.6 multiply_reduce_fusion
  137.8 19.7 %all_to_all.46 = bf16[1,64,32]{2,0,1:T(2,128)(2,1)S(1)} all-to-all(bf16[1,64,32]{2,0,1:T(2,128)(2,1)S(1)} %all_to_all.41), channel_id=1, replica_groups=mesh['kv'=8,'pool'=64] {'pool'}, dimensions={1} | all-to-all | bytes 8192 | tf_op jit(solution)/shard_map/all_to_all | solution.py:135
  157.8 0.6 copy-done.6
  158.7 0.5 broadcast.240
  159.2 0.8 reduce.13
  160.1 24.5 %all_to_all.47 = bf16[64,2,1024]{2,1,0:T(2,128)(2,1)S(1)} all-to-all(bf16[64,2,1024]{2,1,0:T(2,128)(2,1)S(1)} %reshape.527), channel_id=1, replica_groups=mesh['kv'=8,'pool'=64] {'pool'}, dimensions={0} | all-to-all | bytes 524288 | tf_op jit(solution)/shard_map/all_to_all | solution.py:141
  184.8 0.5 convert_reduce_fusion
  185.4 80.0 %all-gather.1 = bf16[64,1,1024]{2,1,0:T(2,128)(2,1)S(1)} all-gather(bf16[1,1,1024]{2,1,0:T(2,128)(2,1)S(1)} %bitcast.109), channel_id=1, replica_groups=mesh['kv'=8,'pool'=64] {'pool'}, dimensions={0}, use_global_device_ids=true | all-gather | bytes 133120 | tf_op jit(solution)/shard_map/all_gather | solution.py:147
  265.5 23.6 %psum.15 = bf16[64,32]{0,1:T(8,128)(2,1)S(1)} all-reduce(f32[64,32]{0,1:T(8,128)S(1)} %fusion.19), channel_id=1, replica_groups=mesh['kv'=8,'pool'=64] {'kv'}, use_global_device_ids=true, to_apply=%region_10.11 | all-reduce | flops 2048 | bytes 12288 | tf_op jit(solution)/shard_map/psum | solution.py:151
  289.2 21.4 %all_to_all.48 = bf16[64,1,32]{2,1,0:T(2,128)(2,1)S(1)} all-to-all(bf16[64,1,32]{2,1,0:T(2,128)(2,1)S(1)} %copy.54), channel_id=1, replica_groups=mesh['kv'=8,'pool'=64] {'pool'}, dimensions={0} | all-to-all | bytes 8192 | tf_op jit(solution)/shard_map/all_to_all | solution.py:152
  310.8 0.6 add_convert_fusion
  (77 shorter events, 5.6 us)
Async XLA Ops:
  0.0 123.4 %copy-start = (bf16[256,2048]{1,0:T(8,128)(2,1)S(1)}, bf16[256,2048]{1,0:T(8,128)(2,1)}, u32[]{:S(2)}) copy-start(bf16[256,2048]{1,0:T(8,128)(2,1)} %param.16) | copy-start | bytes 3145732
  0.0 0.7 copy-start.9
  0.7 2.0 copy-start.7
  0.8 2.0 copy-start.4
  0.8 0.7 copy-start.1
  0.8 94.0 %copy-start.3 = (bf16[2,16,128,128]{3,2,1,0:T(8,128)(2,1)S(1)}, bf16[2,16,128,128]{3,2,1,0:T(8,128)(2,1)}, u32[]{:S(2)}) copy-start(bf16[2,16,128,128]{3,2,1,0:T(8,128)(2,1)} %param.17) | copy-start | bytes 3145732
  96.2 11.5 %copy-start.2 = (bf16[2,2048,128]{2,1,0:T(8,128)(2,1)S(1)}, bf16[2,2048,128]{2,1,0:T(8,128)(2,1)}, u32[]{:S(2)}) copy-start(bf16[2,2048,128]{2,1,0:T(8,128)(2,1)} %param.15) | copy-start | bytes 3145732
  97.3 24.6 %all-to-all-start = ((f32[64,1,512]{2,1,0:T(1,128)}), f32[64,1,512]{2,1,0:T(1,128)S(1)}, u32[]{:S(2)}, u32[]{:S(2)}) async-start(f32[64,1,512]{2,1,0:T(1,128)} %all_to_all.40), calls=%async_computation | async-start | bytes 262144 | tf_op jit(solution)/shard_map/all_to_all | solution.py:103
  108.1 0.7 copy-start.8
  137.7 19.9 %copy-start.5 = (bf16[32,1024]{1,0:T(8,128)(2,1)S(1)}, bf16[32,1024]{1,0:T(8,128)(2,1)}, u32[]{:S(2)}) copy-start(bf16[32,1024]{1,0:T(8,128)(2,1)} %param.21) | copy-start | bytes 196612
  157.6 0.9 copy-start.6
  185.3 80.0 %copy-start.10 = (bf16[1024,32]{0,1:T(8,128)(2,1)S(1)}, bf16[1024,32]{0,1:T(8,128)(2,1)}, u32[]{:S(2)}) copy-start(bf16[1024,32]{0,1:T(8,128)(2,1)} %param.23) | copy-start | bytes 196612
where the time goes:
time: 312 us; the launch traced here: 311 us
  blocking collectives  270 us (87%)
  waiting for transfers between devices  13 us (4%)
  starting transfers between devices  10.4 us (3%)
  local copies, waits for them, and re-layouts  6.74 us (2%)
  other arithmetic  5.5 us (2%)
  matrix products  3.47 us (1%)
    all_gather x1, blocking collectives, per_device(): lax.all_gather(query_rows.reshape(home_rows, query_heads * HEAD_SIZE), 'p...  88.1 us
    all_gather x1, blocking collectives, per_device(): lax.all_gather(activation, 'pool', axis=0, tiled=True)  80 us
    all_to_all x1, blocking collectives, per_device(): lax.all_to_all(sent, 'pool', split_axis=0, concat_axis=0, tiled=True)  24.5 us
    psum x1, blocking collectives, per_device(): mlp_out = narrow_rows(lax.psum(projected_down, 'kv'))  23.6 us
    all_to_all x1, blocking collectives, per_device(): lax.all_to_all(mlp_out, 'pool', split_axis=0, concat_axis=1, tiled=True)  21.4 us
    all_to_all x1, blocking collectives, per_device(): lax.all_to_all(mlp_in, 'pool', split_axis=1, concat_axis=0, tiled=True)  19.7 us
    all_to_all x1, waiting for transfers between devices, per_device(): lax.all_to_all(packed, 'pool', split_axis=0, concat_axis=0, tiled=True)  13 us
    psum x1, blocking collectives, per_device(): lax.psum(jnp.dot(attended, wo, preferred_element_type=jnp.float32), 'kv')  12.6 us
  transfers between devices with their start and end apart: 1, of which 1 were waited for; matrix products, arithmetic and copies ran while one was open for 0% of the time, Pallas kernels for 0%

commit v1 on v0

--- a/solution.py
+++ b/solution.py
@@ -60,8 +60,16 @@
     fresh_values = narrow_rows(
         jnp.dot(normed_input, wkv[1], preferred_element_type=jnp.float32)
     ).reshape(home_rows, shared_heads, HEAD_SIZE)
-    every_query = lax.all_gather(
-        query_rows.reshape(home_rows, query_heads * HEAD_SIZE), "pool", axis=0, tiled=True
+    every_query = jnp.concatenate(
+        lax.all_to_all(
+            jnp.stack(
+                [query_rows.reshape(home_rows, query_heads * HEAD_SIZE)] * lax.axis_size("pool")
+            ),
+            "pool",
+            0,
+            0,
+        ),
+        axis=0,
     )
     request_list = every_query.shape[0]
     every_query = every_query.reshape(request_list, shared_heads, queries_per_shared, HEAD_SIZE)

time: 312 us -> 252 us (0.81)
  blocking collectives: 270 us -> 182 us
  starting transfers between devices: 10.4 us -> 24.1 us
  waiting for transfers between devices: 13 us -> 25.9 us
    all_gather x1 -> x0, blocking collectives: 88.1 us -> none  [per_device(): lax.all_gather(query_rows.reshape(home_rows, query_heads * HEAD_SIZE), 'p...]
    all_to_all x0 -> x1, starting transfers between devices: none -> 18.7 us  [per_device(): lax.all_to_all(jnp.stack([query_rows.reshape(home_rows, query_heads * HEA...]
    all_to_all x0 -> x1, waiting for transfers between devices: none -> 11.4 us  [per_device(): lax.all_to_all(jnp.stack([query_rows.reshape(home_rows, query_heads * HEA...]
    all_to_all x1, starting transfers between devices: 10.4 us -> 5.4 us  [per_device(): lax.all_to_all(packed, 'pool', split_axis=0, concat_axis=0, tiled=True)]
  transfers between devices with their start and end apart: 1 -> 2, of which waited for: 1 -> 2; matrix products, arithmetic and copies ran while one was open for 0% -> 1% of each run, Pallas kernels for 0% -> 0%
where the time goes in v1:
time: 252 us
  blocking collectives  182 us (72%)
  waiting for transfers between devices  25.9 us (10%)
  starting transfers between devices  24.1 us (10%)
  local copies, waits for them, and re-layouts  7.43 us (3%)
  other arithmetic  6.4 us (3%)
  matrix products  3.47 us (1%)
    all_gather x1, blocking collectives, per_device(): lax.all_gather(activation, 'pool', axis=0, tiled=True)  80.1 us
    psum x1, blocking collectives, per_device(): mlp_out = narrow_rows(lax.psum(projected_down, 'kv'))  23.6 us
    all_to_all x1, blocking collectives, per_device(): lax.all_to_all(sent, 'pool', split_axis=0, concat_axis=0, tiled=True)  23.5 us
    all_to_all x1, blocking collectives, per_device(): lax.all_to_all(mlp_out, 'pool', split_axis=0, concat_axis=1, tiled=True)  21.3 us
    all_to_all x1, blocking collectives, per_device(): lax.all_to_all(mlp_in, 'pool', split_axis=1, concat_axis=0, tiled=True)  20.6 us
    all_to_all x1, starting transfers between devices, per_device(): lax.all_to_all(jnp.stack([query_rows.reshape(home_rows, query_heads * HEA...  18.7 us
    all_to_all x1, waiting for transfers between devices, per_device(): lax.all_to_all(packed, 'pool', split_axis=0, concat_axis=0, tiled=True)  14.5 us
    psum x1, blocking collectives, per_device(): lax.psum(jnp.dot(attended, wo, preferred_element_type=jnp.float32), 'kv')  12.6 us
  transfers between devices with their start and end apart: 2, of which 2 were waited for; matrix products, arithmetic and copies ran while one was open for 1% of the time, Pallas kernels for 0%

profile of v1, /device:TPU:8, one launch (start us, length us, event | category | flops | bytes accessed | tf_op | source)
XLA Modules:
  0.0 251.6 jit_solution(14879176266495623159)
XLA Ops:
  0.0 0.8 copy-done.4
  0.8 0.6 multiply_reduce_fusion.1
  2.1 0.6 copy-done.1
  2.8 0.6 dynamic_slice.3
  4.1 1.5 fusion.4
  6.3 0.8 reduce.13
  7.1 0.6 reshape.523
  7.8 18.7 %all-to-all-start = ((bf16[64,2,128]{2,1,0:T(2,128)(2,1)}), bf16[64,2,128]{2,1,0:T(2,128)(2,1)S(1)}, u32[]{:S(2)}, u32[]{:S(2)}) async-start(bf16[64,2,128]{2,1,0:T(2,128)(2,1)} %reshape.523), calls=%async_computation | async-start | bytes 65536 | tf_op jit(solution)/shard_map/all_to_all | solution.py:64
  27.0 0.7 gather_fusion
  27.8 0.5 copy-done.8
  28.6 11.4 %all-to-all-done = bf16[64,2,128]{2,1,0:T(2,128)(2,1)S(1)} async-done(((bf16[64,2,128]{2,1,0:T(2,128)(2,1)}), bf16[64,2,128]{2,1,0:T(2,128)(2,1)S(1)}, u32[]{:S(2)}, u32[]{:S(2)}) %all-to-all-start) | async-done | bytes 32800 | tf_op jit(solution)/shard_map/all_to_all | solution.py:64
  41.7 0.8 all_to_all.44
  42.5 5.4 %all-to-all-start.1 = ((f32[64,1,512]{2,1,0:T(1,128)}), f32[64,1,512]{2,1,0:T(1,128)S(1)}, u32[]{:S(2)}, u32[]{:S(2)}) async-start(f32[64,1,512]{2,1,0:T(1,128)} %all_to_all.44), calls=%async_computation.1 | async-start | bytes 262144 | tf_op jit(solution)/shard_map/all_to_all | solution.py:111
  48.0 14.5 %all-to-all-done.1 = f32[64,1,512]{2,1,0:T(1,128)S(1)} async-done(((f32[64,1,512]{2,1,0:T(1,128)}), f32[64,1,512]{2,1,0:T(1,128)S(1)}, u32[]{:S(2)}, u32[]{:S(2)}) %all-to-all-start.1) | async-done | bytes 131104 | tf_op jit(solution)/shard_map/all_to_all | solution.py:111
  64.2 12.6 %psum.14 = f32[1,2048]{1,0:T(1,128)S(1)} all-reduce(f32[1,2048]{1,0:T(1,128)S(1)} %fusion.53), channel_id=1, replica_groups=mesh['kv'=8,'pool'=64] {'kv'}, use_global_device_ids=true, to_apply=%region_7.8 | all-reduce | flops 2048 | bytes 16384 | tf_op jit(solution)/shard_map/psum | solution.py:140
  76.9 0.7 multiply_reduce_fusion
  78.5 20.6 %all_to_all.51 = bf16[1,64,32]{2,0,1:T(2,128)(2,1)S(1)} all-to-all(bf16[1,64,32]{2,0,1:T(2,128)(2,1)S(1)} %all_to_all.45), channel_id=1, replica_groups=mesh['kv'=8,'pool'=64] {'pool'}, dimensions={1} | all-to-all | bytes 8192 | tf_op jit(solution)/shard_map/all_to_all | solution.py:143
  99.4 0.6 copy-done.6
  100.3 0.8 reduce.14
  101.2 23.5 %all_to_all.52 = bf16[64,2,1024]{2,1,0:T(2,128)(2,1)S(1)} all-to-all(bf16[64,2,1024]{2,1,0:T(2,128)(2,1)S(1)} %reshape.525), channel_id=1, replica_groups=mesh['kv'=8,'pool'=64] {'pool'}, dimensions={0} | all-to-all | bytes 524288 | tf_op jit(solution)/shard_map/all_to_all | solution.py:149
  125.5 80.1 %all-gather = bf16[64,1,1024]{2,1,0:T(2,128)(2,1)S(1)} all-gather(bf16[1,1,1024]{2,1,0:T(2,128)(2,1)S(1)} %bitcast.110), channel_id=1, replica_groups=mesh['kv'=8,'pool'=64] {'pool'}, dimensions={0}, use_global_device_ids=true | all-gather | bytes 133120 | tf_op jit(solution)/shard_map/all_gather | solution.py:155
  205.8 23.6 %psum.15 = bf16[64,32]{0,1:T(8,128)(2,1)S(1)} all-reduce(f32[64,32]{0,1:T(8,128)S(1)} %fusion.19), channel_id=1, replica_groups=mesh['kv'=8,'pool'=64] {'kv'}, use_global_device_ids=true, to_apply=%region_10.11 | all-reduce | flops 2048 | bytes 12288 | tf_op jit(solution)/shard_map/psum | solution.py:159
  229.5 21.3 %all_to_all.53 = bf16[64,1,32]{2,1,0:T(2,128)(2,1)S(1)} all-to-all(bf16[64,1,32]{2,1,0:T(2,128)(2,1)S(1)} %copy.66), channel_id=1, replica_groups=mesh['kv'=8,'pool'=64] {'pool'}, dimensions={0} | all-to-all | bytes 8192 | tf_op jit(solution)/shard_map/all_to_all | solution.py:160
  251.0 0.6 add_convert_fusion
  (81 shorter events, 7.0 us)
Async XLA Ops:
  0.0 64.0 %copy-start = (bf16[256,2048]{1,0:T(8,128)(2,1)S(1)}, bf16[256,2048]{1,0:T(8,128)(2,1)}, u32[]{:S(2)}) copy-start(bf16[256,2048]{1,0:T(8,128)(2,1)} %param.16) | copy-start | bytes 3145732
  0.0 0.8 copy-start.4
  2.1 2.0 copy-start.7
  2.1 0.7 copy-start.1
  2.1 24.4 %copy-start.2 = (bf16[2,2048,128]{2,1,0:T(8,128)(2,1)S(1)}, bf16[2,2048,128]{2,1,0:T(8,128)(2,1)}, u32[]{:S(2)}) copy-start(bf16[2,2048,128]{2,1,0:T(8,128)(2,1)} %param.15) | copy-start | bytes 3145732
  4.1 22.4 %copy-start.9 = (s32[16]{0:T(128)S(1)}, s32[16]{0:T(128)}, u32[]{:S(2)}) copy-start(s32[16]{0:T(128)} %param.18) | copy-start | bytes 196
  5.6 22.8 %copy-start.3 = (bf16[2,16,128,128]{3,2,1,0:T(8,128)(2,1)S(1)}, bf16[2,16,128,128]{3,2,1,0:T(8,128)(2,1)}, u32[]{:S(2)}) copy-start(bf16[2,16,128,128]{3,2,1,0:T(8,128)(2,1)} %param.17) | copy-start | bytes 3145732
  7.8 32.2 %all-to-all-start = ((bf16[64,2,128]{2,1,0:T(2,128)(2,1)}), bf16[64,2,128]{2,1,0:T(2,128)(2,1)S(1)}, u32[]{:S(2)}, u32[]{:S(2)}) async-start(bf16[64,2,128]{2,1,0:T(2,128)(2,1)} %reshape.523), calls=%async_computation | async-start | bytes 65536 | tf_op jit(solution)/shard_map/all_to_all | solution.py:64
  27.7 0.7 copy-start.8
  42.5 20.0 %all-to-all-start.1 = ((f32[64,1,512]{2,1,0:T(1,128)}), f32[64,1,512]{2,1,0:T(1,128)S(1)}, u32[]{:S(2)}, u32[]{:S(2)}) async-start(f32[64,1,512]{2,1,0:T(1,128)} %all_to_all.44), calls=%async_computation.1 | async-start | bytes 262144 | tf_op jit(solution)/shard_map/all_to_all | solution.py:111
  78.4 20.8 %copy-start.5 = (bf16[32,1024]{1,0:T(8,128)(2,1)S(1)}, bf16[32,1024]{1,0:T(8,128)(2,1)}, u32[]{:S(2)}) copy-start(bf16[32,1024]{1,0:T(8,128)(2,1)} %param.22) | copy-start | bytes 196612
  99.2 0.9 copy-start.6
  125.5 80.1 %copy-start.10 = (bf16[1024,32]{0,1:T(8,128)(2,1)S(1)}, bf16[1024,32]{0,1:T(8,128)(2,1)}, u32[]{:S(2)}) copy-start(bf16[1024,32]{0,1:T(8,128)(2,1)} %param.23) | copy-start | bytes 196612
